TPU v7x, 32 devices: a whole 2x2x4 slice. The times are simulated.
32 devices in a mesh: dp: 8 (over z, x), mp: 4 (over y, core).
Axes of the slice: x: 2, y: 2, z: 4, core: 2. Of those that a mesh axis runs over, the one named last changes fastest.
Arguments:
- media: bfloat16 [16, 8, 256, 1024], P('dp'), may hold values from -6 to 6
- latents: bfloat16 [64, 1024], replicated, may hold values from -6 to 6
- time_embed: bfloat16 [8, 1024], replicated, may hold values from -5 to 5
- media_gain: float32 [2, 1024], replicated, may hold values from 0.25 to 1.75
- latent_gain: float32 [2, 1024], replicated, may hold values from 0.25 to 1.75
- ffn_gain: float32 [2, 1024], replicated, may hold values from 0.25 to 1.75
- out_gain: float32 [1024], replicated, may hold values from 0.25 to 1.75
- w_query: bfloat16 [2, 1024, 512], P(None, 'dp', 'mp'), may hold values from -0.1875 to 0.1875
- w_key: bfloat16 [2, 1024, 512], P(None, 'dp', 'mp'), may hold values from -0.1875 to 0.1875
- w_value: bfloat16 [2, 1024, 512], P(None, 'dp', 'mp'), may hold values from -0.1875 to 0.1875
- w_out: bfloat16 [2, 512, 1024], P(None, 'mp', 'dp'), may hold values from -0.25 to 0.25
- w_up: bfloat16 [2, 1024, 4096], P(None, 'dp', 'mp'), may hold values from -0.1875 to 0.1875
- w_down: bfloat16 [2, 4096, 1024], P(None, 'mp', 'dp'), may hold values from -0.09375 to 0.09375
Outputs:
- resampled: bfloat16 [16, 64, 1024], P('dp')
All inputs are finite; a program needn't handle non-finite values.
Results may differ from a plain program's by a relative error of at most 0.013.
Values may be sent and summed in bfloat16 or wider, within the bound.
A program may use at most 128 MiB of HBM per device.

v0:
```python
import jax
import jax.numpy as jnp
from jax import lax
from jax.sharding import PartitionSpec as P

HEAD = 64
LAYERS = 2


def layer_norm(values, gain):
    center = values - jnp.mean(values, axis=-1, keepdims=True)
    spread = jnp.mean(center * center, axis=-1, keepdims=True)
    return center * lax.rsqrt(spread + 1e-05) * gain


def matmul(left, right):
    return jnp.dot(left, right, preferred_element_type=jnp.float32)


def on_device(
    media,
    latents,
    time_embed,
    media_gain,
    latent_gain,
    ffn_gain,
    out_gain,
    w_query,
    w_key,
    w_value,
    w_out,
    w_up,
    w_down,
):
    samples = media.shape[0]
    frames = media.shape[1]
    patches = media.shape[2]
    width = media.shape[3]
    count = latents.shape[0]
    head_size = HEAD
    local_heads = w_query.shape[2] // head_size
    scale = head_size ** (-0.5)
    tokens = frames * patches
    flat = (media.astype(jnp.float32) + time_embed.astype(jnp.float32)[None, :, None, :]).reshape(
        samples * tokens, width
    )
    state = jnp.broadcast_to(latents.astype(jnp.float32)[None], (samples, count, width)).reshape(
        samples * count, width
    )
    row_parts = (
        lax.all_gather(w_query, "dp", axis=1, tiled=True),
        lax.all_gather(w_key, "dp", axis=1, tiled=True),
        lax.all_gather(w_value, "dp", axis=1, tiled=True),
        lax.all_gather(w_up, "dp", axis=1, tiled=True),
    )
    col_parts = (
        lax.all_gather(w_out, "dp", axis=2, tiled=True),
        lax.all_gather(w_down, "dp", axis=2, tiled=True),
    )

    def full_rows(values, gain):
        normed = layer_norm(values, gain).astype(jnp.bfloat16)
        return normed

    def add_update(current, partial_value):
        return current + lax.psum(partial_value.astype(jnp.bfloat16), "mp").astype(jnp.float32)

    for layer in range(LAYERS):
        query_weight = row_parts[0][layer]
        key_weight = row_parts[1][layer]
        value_weight = row_parts[2][layer]
        up_weight = row_parts[3][layer]
        out_weight = col_parts[0][layer]
        down_weight = col_parts[1][layer]
        media_normed = layer_norm(flat, media_gain[layer]).astype(jnp.bfloat16)
        latent_normed = full_rows(state, latent_gain[layer])
        query = matmul(latent_normed, query_weight)
        key_media = matmul(media_normed, key_weight)
        value_media = matmul(media_normed, value_weight)
        key_latent = matmul(latent_normed, key_weight)
        value_latent = matmul(latent_normed, value_weight)
        queries = (
            (query * scale).astype(jnp.bfloat16).reshape(samples, count, local_heads, head_size)
        )
        keys = jnp.concatenate(
            [
                key_media.astype(jnp.bfloat16).reshape(samples, tokens, local_heads, head_size),
                key_latent.astype(jnp.bfloat16).reshape(samples, count, local_heads, head_size),
            ],
            axis=1,
        )
        values = jnp.concatenate(
            [
                value_media.astype(jnp.bfloat16).reshape(samples, tokens, local_heads, head_size),
                value_latent.astype(jnp.bfloat16).reshape(samples, count, local_heads, head_size),
            ],
            axis=1,
        )
        scores = jnp.einsum("sqhd,skhd->shqk", queries, keys, preferred_element_type=jnp.float32)
        probs = jax.nn.softmax(scores, axis=-1).astype(jnp.bfloat16)
        attended = jnp.einsum("shqk,skhd->sqhd", probs, values, preferred_element_type=jnp.float32)
        attended = attended.astype(jnp.bfloat16).reshape(samples * count, local_heads * head_size)
        state = add_update(state, matmul(attended, out_weight))
        ffn_normed = full_rows(state, ffn_gain[layer])
        hidden = jax.nn.gelu(matmul(ffn_normed, up_weight), approximate=False).astype(jnp.bfloat16)
        state = add_update(state, matmul(hidden, down_weight))
    final = layer_norm(state, out_gain).astype(jnp.bfloat16)
    return final.reshape(samples, count, width)


def solution(mesh):
    in_specs = (
        P("dp", None, None, None),
        P(),
        P(),
        P(),
        P(),
        P(),
        P(),
        P(None, "dp", "mp"),
        P(None, "dp", "mp"),
        P(None, "dp", "mp"),
        P(None, "mp", "dp"),
        P(None, "dp", "mp"),
        P(None, "mp", "dp"),
    )
    out_specs = P("dp", None, None)
    return jax.shard_map(
        on_device, mesh=mesh, in_specs=in_specs, out_specs=out_specs, check_vma=False
    )
```

profile of v0, /device:TPU:0, one launch (start us, length us, event | category | flops | bytes accessed | tf_op | source)
XLA Modules:
  0.0 459.3 jit_solution(7624220394603291275)
XLA Ops:
  7.4 0.9 convert_element_type.133
  8.3 1.0 convert_reduce_fusion
  9.3 0.2 fusion.33
  9.5 0.8 fusion.217
  10.3 33.3 %all_gather.20 = bf16[2,1024,128]{2,1,0:T(8,128)(2,1)S(1)} all-gather(bf16[2,128,128]{2,1,0:T(8,128)(2,1)} %param.21), channel_id=1, replica_groups=mesh['dp'=8,'mp'=4] {'dp'}, dimensions={1}, use_global_device_ids=true | all-gather | bytes 589824 | tf_op jit(solution)/shard_map/all_gather | solution.py:52
  43.6 0.7 convert_element_type.135
  44.3 5.3 %fusion.3 = f32[2,8,256]{2,1,0:T(8,128)S(1)} fusion(bf16[2,8,256,1024]{3,2,1,0:T(8,128)(2,1)} %param.13, f32[8,1024]{1,0:T(8,128)S(1)} %convert_element_type.135), kind=kLoop, calls=%fused_computation.7 | loop fusion | flops 12578816 | bytes 8437760 | tf_op jit(solution)/shard_map/reduce_sum | solution.py:11
  49.6 0.5 copy-done
  50.1 3.2 multiply_reduce_fusion
  53.3 0.1 fusion.35
  53.5 0.2 convolution_convert_fusion.10
  53.7 5.8 %multiply_convert_fusion = (bf16[2,8,256,1024]{3,2,1,0:T(8,128)(2,1)}, bf16[2,8,256,1024]{3,2,1,0:T(8,128)(2,1)S(1)}) fusion(bf16[2,8,256,1024]{3,2,1,0:T(8,128)(2,1)S(1)} %copy-done, f32[1024]{0:T(1024)S(1)} %bitcast.110, f32[2,8,256]{2,1,0:T(8,128)S(1)} %add_rsqrt_fusion, f32[2,8,256]{2,1,0:T(8,128)S(1)} %broadcast_multiply_fusion, ...), kind=kLoop, calls=%fused_computation.2 | loop fusion | flops 33554432 | bytes 25239552 | tf_op jit(solution)/shard_map/convert_element_type | solution.py:75
  59.4 3.4 convolution_convert_fusion.2
  62.9 31.3 %all_gather.18 = bf16[2,1024,128]{2,1,0:T(8,128)(2,1)S(1)} all-gather(bf16[2,128,128]{2,1,0:T(8,128)(2,1)S(1)} %copy-done.12), channel_id=1, replica_groups=mesh['dp'=8,'mp'=4] {'dp'}, dimensions={1}, use_global_device_ids=true | all-gather | bytes 589824 | tf_op jit(solution)/shard_map/all_gather | solution.py:53
  94.1 0.2 convolution_convert_fusion.11
  94.4 0.6 copy-done.3
  94.9 3.5 convolution_convert_fusion.3
  98.5 0.1 copy.29
  98.6 31.6 %all_gather.19 = bf16[2,1024,128]{2,1,0:T(8,128)(2,1)S(1)} all-gather(bf16[2,128,128]{2,1,0:T(8,128)(2,1)S(1)} %copy-done.13), channel_id=1, replica_groups=mesh['dp'=8,'mp'=4] {'dp'}, dimensions={1}, use_global_device_ids=true | all-gather | bytes 589824 | tf_op jit(solution)/shard_map/all_gather | solution.py:51
  130.2 0.2 fusion.17
  130.4 0.6 copy-done.10
  131.1 3.9 reshape.424
  135.0 3.5 copy.28
  138.7 3.9 reshape.423
  142.6 3.5 copy.25
  146.2 3.3 fusion.218
  149.5 2.2 fusion.15
  151.9 27.0 %all_gather.21 = bf16[2,128,1024]{2,1,0:T(8,128)(2,1)S(1)} all-gather(bf16[2,128,128]{2,1,0:T(8,128)(2,1)S(1)} %copy-done.14), channel_id=1, replica_groups=mesh['dp'=8,'mp'=4] {'dp'}, dimensions={2}, use_global_device_ids=true | all-gather | bytes 589824 | tf_op jit(solution)/shard_map/all_gather | solution.py:57
  179.0 0.8 copy-done.6
  179.8 0.9 convolution_convert_fusion.5
  180.8 0.5 all-gather.3.cloned.1.call-update
  181.3 0.5 all-gather.5.cloned.1.call-update
  182.0 6.8 %convolution_convert_fusion = bf16[4096,128]{1,0:T(8,128)(2,1)} fusion(bf16[4096,1024]{1,0:T(8,128)(2,1)} %bitcast.100, bf16[2,1024,128]{2,1,0:T(8,128)(2,1)S(1)} %all_gather.20), kind=kOutput, calls=%fused_computation.9 | convolution fusion | flops 1074266112 | bytes 9699328 | tf_op jit(solution)/shard_map/dot_general | solution.py:17
  188.7 23.7 %all-reduce.5.cloned.1.call-done = bf16[128,1024]{1,0:T(8,128)(2,1)} async-done(((bf16[128,1024]{1,0:T(8,128)(2,1)}), bf16[128,1024]{1,0:T(8,128)(2,1)}) %all-reduce.5.cloned.1.call-update) | async-done | bytes 262160 | tf_op jit(solution)/shard_map/psum | solution.py:66
  212.5 1.1 fusion.55
  213.6 1.2 multiply_reduce_fusion.4
  214.7 1.1 multiply_convert_fusion.5
  215.9 39.4 %all-gather.3.cloned.1.call-done = bf16[2,1024,1024]{2,1,0:T(8,128)(2,1)} async-done(((bf16[2,128,1024]{2,1,0:T(8,128)(2,1)}), bf16[2,1024,1024]{2,1,0:T(8,128)(2,1)}) %all-gather.3.cloned.1.call-update) | async-done | bytes 4194320 | tf_op jit(solution)/shard_map/all_gather | solution.py:54
  255.3 75.0 %all-gather.5.cloned.1.call-done = bf16[2,1024,1024]{2,1,0:T(8,128)(2,1)} async-done(((bf16[2,1024,128]{2,1,0:T(8,128)(2,1)}), bf16[2,1024,1024]{2,1,0:T(8,128)(2,1)}) %all-gather.5.cloned.1.call-update) | async-done | bytes 4194320 | tf_op jit(solution)/shard_map/all_gather | solution.py:58
  330.3 4.8 %fusion.13 = bf16[128,1024]{1,0:T(8,128)(2,1)} fusion(bf16[2,1024,1024]{2,1,0:T(8,128)(2,1)} %all-gather.5.cloned.1.call-done, bf16[128,1024]{1,0:T(8,128)(2,1)S(1)} %multiply_convert_fusion.5, bf16[2,1024,1024]{2,1,0:T(8,128)(2,1)} %all-gather.3.cloned.1.call-done), kind=kOutput, calls=%fused_computation.27 | convolution fusion | flops 545521664 | bytes 4718592 | tf_op jit(solution)/shard_map/dot_general | solution.py:17
  335.1 0.3 all-reduce.9.cloned.1.call-start
  335.4 6.7 %convolution_convert_fusion.1 = bf16[4096,128]{1,0:T(8,128)(2,1)} fusion(bf16[4096,1024]{1,0:T(8,128)(2,1)} %bitcast.101, bf16[2,1024,128]{2,1,0:T(8,128)(2,1)S(1)} %copy-done.4), kind=kOutput, calls=%fused_computation.10 | convolution fusion | flops 1074266112 | bytes 9699328 | tf_op jit(solution)/shard_map/dot_general | solution.py:17
  342.1 3.9 reshape.426
  346.0 3.5 copy.36
  349.5 3.9 reshape.425
  353.4 3.6 copy.33
  357.0 8.7 %all-reduce.7.cloned.1.call-done = bf16[128,1024]{1,0:T(8,128)(2,1)} async-done(((bf16[128,1024]{1,0:T(8,128)(2,1)}), bf16[128,1024]{1,0:T(8,128)(2,1)}) %all-reduce.7.cloned.1.call-update) | async-done | bytes 262160 | tf_op jit(solution)/shard_map/psum | solution.py:66
  365.7 1.1 fusion.58
  366.8 1.2 multiply_reduce_fusion.3
  368.0 1.1 multiply_convert_fusion.4
  369.1 0.2 convolution_convert_fusion.8
  369.3 0.2 fusion.18
  369.6 0.2 convolution_convert_fusion.9
  370.3 3.2 fusion.223
  373.6 2.2 fusion.16
  376.0 0.9 convolution_convert_fusion.4
  377.0 32.4 %all-reduce.9.cloned.1.call-done = bf16[128,1024]{1,0:T(8,128)(2,1)} async-done(((bf16[128,1024]{1,0:T(8,128)(2,1)}), bf16[128,1024]{1,0:T(8,128)(2,1)}) %all-reduce.9.cloned.1.call-update) | async-done | bytes 262160 | tf_op jit(solution)/shard_map/psum | solution.py:66
  409.4 1.1 fusion.214
  410.6 0.2 multiply_reduce_fusion.2
  410.8 4.9 %fusion.14 = bf16[128,1024]{1,0:T(8,128)(2,1)} fusion(bf16[2,1024,1024]{2,1,0:T(8,128)(2,1)} %all-gather.5.cloned.1.call-done, bf16[2,1024,1024]{2,1,0:T(8,128)(2,1)} %all-gather.3.cloned.1.call-done, f32[128,1024]{1,0:T(8,128)S(1)} %get-tuple-element.6, f32[1024]{0:T(1024)S(1)} %bitcast.112, f32[128]{0:T(128)S(1)} %add_rsqrt_fusion.3, ...), kind=kOutput, calls=%fused_computation.28 | convolution fusion | flops 546045952 | bytes 4985856 | tf_op jit(solution)/shard_map/dot_general | solution.py:17
  415.7 32.4 %all-reduce.11.cloned.1.call-done = bf16[128,1024]{1,0:T(8,128)(2,1)} async-done(((bf16[128,1024]{1,0:T(8,128)(2,1)}), bf16[128,1024]{1,0:T(8,128)(2,1)}) %all-reduce.11.cloned.1.call-update) | async-done | bytes 262160 | tf_op jit(solution)/shard_map/psum | solution.py:66
  448.1 1.1 fusion.129
  449.2 1.1 multiply_reduce_fusion.1
  450.4 1.8 multiply_convert_fusion.2
  (68 shorter events, 1.6 us)
Async XLA Ops:
  7.4 205.1 %all-reduce.5.cloned.1.call-start = ((), (), s32[]{:S(2)}) async-start(), calls=%async_computation | async-start | bytes 524288 | tf_op jit(solution)/shard_map/psum | solution.py:66
  44.3 5.8 %copy-start = (bf16[2,8,256,1024]{3,2,1,0:T(8,128)(2,1)S(1)}, bf16[2,8,256,1024]{3,2,1,0:T(8,128)(2,1)}, u32[]{:S(2)}) copy-start(bf16[2,8,256,1024]{3,2,1,0:T(8,128)(2,1)} %param.13) | copy-start | bytes 25165828
  50.1 3.2 copy-start.15
  59.4 3.4 copy-start.12
  94.1 0.8 copy-start.3
  94.9 3.7 copy-start.13
  130.2 0.8 copy-start.10
  146.1 3.4 copy-start.9
  149.5 2.4 copy-start.14
  151.7 30.2 %copy-start.16 = (f32[2,1024]{1,0:T(2,128)S(1)}, f32[2,1024]{1,0:T(2,128)}, u32[]{:S(2)}) copy-start(f32[2,1024]{1,0:T(2,128)} %param.18) | copy-start | bytes 24580
  179.0 0.8 copy-start.6
  180.7 74.5 %all-gather.3.cloned.1.call-start = ((), (), s32[]{:S(2)}) async-start(), calls=%async_computation.1 | async-start | bytes 4718592 | tf_op jit(solution)/shard_map/all_gather | solution.py:54
  181.3 149.0 %all-gather.5.cloned.1.call-start = ((), (), s32[]{:S(2)}) async-start(), calls=%async_computation.2 | async-start | bytes 4718592 | tf_op jit(solution)/shard_map/all_gather | solution.py:58
  181.9 183.8 %all-reduce.7.cloned.1.call-start = ((), (), s32[]{:S(2)}) async-start(), calls=%async_computation.3 | async-start | bytes 524288 | tf_op jit(solution)/shard_map/psum | solution.py:66
  215.9 119.5 %copy-start.4 = (bf16[2,1024,128]{2,1,0:T(8,128)(2,1)S(1)}, bf16[2,1024,128]{2,1,0:T(8,128)(2,1)}, u32[]{:S(2)}) copy-start(bf16[2,1024,128]{2,1,0:T(8,128)(2,1)} %copy-done.3) | copy-start | bytes 1572868
  335.1 74.3 %all-reduce.9.cloned.1.call-start = ((), (), s32[]{:S(2)}) async-start(), calls=%async_computation.4 | async-start | bytes 524288 | tf_op jit(solution)/shard_map/psum | solution.py:66
  353.4 12.3 %copy-start.1 = (bf16[128,1024]{1,0:T(8,128)(2,1)S(1)}, bf16[128,1024]{1,0:T(8,128)(2,1)}, u32[]{:S(2)}) copy-start(bf16[128,1024]{1,0:T(8,128)(2,1)} %all-reduce.5.cloned.1.call-done) | copy-start | bytes 786436
  357.0 12.4 %copy-start.11 = (bf16[2,1024,128]{2,1,0:T(8,128)(2,1)S(1)}, bf16[2,1024,128]{2,1,0:T(8,128)(2,1)}, u32[]{:S(2)}) copy-start(bf16[2,1024,128]{2,1,0:T(8,128)(2,1)} %copy-done.10) | copy-start | bytes 1572868
  357.0 12.6 %copy-start.5 = (bf16[2,1024,128]{2,1,0:T(8,128)(2,1)S(1)}, bf16[2,1024,128]{2,1,0:T(8,128)(2,1)}, u32[]{:S(2)}) copy-start(bf16[2,1024,128]{2,1,0:T(8,128)(2,1)} %copy-done.3) | copy-start | bytes 1572868
  369.8 3.8 copy-start.8
  373.6 2.5 copy-start.7
  373.6 35.9 %copy-start.2 = (bf16[128,1024]{1,0:T(8,128)(2,1)S(1)}, bf16[128,1024]{1,0:T(8,128)(2,1)}, u32[]{:S(2)}) copy-start(bf16[128,1024]{1,0:T(8,128)(2,1)} %all-reduce.7.cloned.1.call-done) | copy-start | bytes 786436
  377.0 71.1 %all-reduce.11.cloned.1.call-start = ((), (), s32[]{:S(2)}) async-start(), calls=%async_computation.5 | async-start | bytes 524288 | tf_op jit(solution)/shard_map/psum | solution.py:66
  410.8 39.6 %copy-start.17 = (f32[1024]{0:T(1024)S(1)}, f32[1024]{0:T(1024)}, u32[]{:S(2)}) copy-start(f32[1024]{0:T(1024)} %param.19) | copy-start | bytes 12292
Sparse Core Ops, SparseCore 0:
  180.8 31.5 all-reduce.4
  335.2 30.4 all-reduce.6
  377.1 32.2 all-reduce.8
  415.8 32.2 all-reduce.10
Sparse Core Ops, SparseCore 1:
  183.4 71.8 all-gather.2
  257.2 73.0 all-gather.4
where the time goes:
time: 460 us; the launch traced here: 459 us
  waiting for transfers between devices  213 us (46%)
  blocking collectives  123 us (27%)
  matrix products  44.2 us (10%)
  local copies, waits for them, and re-layouts  34.3 us (7%)
  other arithmetic  29.4 us (6%)
  between operations  15 us (3%)
    psum x4, waiting for transfers between devices, add_update(): lax.psum(partial_value.astype(jnp.bfloat16), 'mp').astype(jnp.float32)  97.3 us
    all_gather x1, waiting for transfers between devices, on_device(): lax.all_gather(w_down, 'dp', axis=2, tiled=True)  75 us
    all_gather x1, waiting for transfers between devices, on_device(): lax.all_gather(w_up, 'dp', axis=1, tiled=True)  39.4 us
    all_gather x1, blocking collectives, on_device(): lax.all_gather(w_key, 'dp', axis=1, tiled=True)  33.3 us
    dot_general x14, matrix products, matmul(): return jnp.dot(left, right, preferred_element_type=jnp.float32)  33.2 us
    all_gather x1, blocking collectives, on_device(): lax.all_gather(w_query, 'dp', axis=1, tiled=True)  31.6 us
    all_gather x1, blocking collectives, on_device(): lax.all_gather(w_value, 'dp', axis=1, tiled=True)  31.3 us
    all_gather x1, blocking collectives, on_device(): lax.all_gather(w_out, 'dp', axis=2, tiled=True)  27 us
  transfers between devices with their start and end apart: 6, of which 6 were waited for; matrix products, arithmetic and copies ran while one was open for 7% of the time, Pallas kernels for 0%

commit v1 on v0

--- a/solution.py
+++ b/solution.py
@@ -63,7 +63,9 @@
         return normed
 
     def add_update(current, partial_value):
-        return current + lax.psum(partial_value.astype(jnp.bfloat16), "mp").astype(jnp.float32)
+        return current + jnp.sum(
+            lax.all_gather(partial_value.astype(jnp.bfloat16), "mp"), axis=0
+        ).astype(jnp.float32)
 
     for layer in range(LAYERS):
         query_weight = row_parts[0][layer]

time: 460 us -> 436 us (0.948)
  waiting for transfers between devices: 213 us -> 196 us
    psum x4 -> x0, waiting for transfers between devices: 97.3 us -> none  [add_update(): lax.psum(partial_value.astype(jnp.bfloat16), 'mp').astype(jnp.float32)]
    all_gather x0 -> x4, waiting for transfers between devices: none -> 46.5 us  [add_update(): lax.all_gather(partial_value.astype(jnp.bfloat16), 'mp')]
    all_gather x1, waiting for transfers between devices: 39.4 us -> 72.9 us  [on_device(): lax.all_gather(w_up, 'dp', axis=1, tiled=True)]
    reduce_sum x0 -> x4, other arithmetic: none -> 5.77 us  [add_update(): jnp.sum(lax.all_gather(partial_value.astype(jnp.bfloat16), 'mp'), axis=0)]
  transfers between devices with their start and end apart: 6 -> 6, of which waited for: 6 -> 5; matrix products, arithmetic and copies ran while one was open for 7% -> 7% of each run, Pallas kernels for 0% -> 0%
where the time goes in v1:
time: 436 us
  waiting for transfers between devices  196 us (45%)
  blocking collectives  123 us (28%)
  matrix products  42.8 us (10%)
  local copies, waits for them, and re-layouts  33.3 us (8%)
  other arithmetic  25.8 us (6%)
  between operations  13.9 us (3%)
    all_gather x1, waiting for transfers between devices, on_device(): lax.all_gather(w_down, 'dp', axis=2, tiled=True)  75.3 us
    all_gather x1, waiting for transfers between devices, on_device(): lax.all_gather(w_up, 'dp', axis=1, tiled=True)  72.9 us
    all_gather x4, waiting for transfers between devices, add_update(): lax.all_gather(partial_value.astype(jnp.bfloat16), 'mp')  46.5 us
    all_gather x1, blocking collectives, on_device(): lax.all_gather(w_key, 'dp', axis=1, tiled=True)  33.3 us
    dot_general x14, matrix products, matmul(): return jnp.dot(left, right, preferred_element_type=jnp.float32)  32.2 us
    all_gather x1, blocking collectives, on_device(): lax.all_gather(w_query, 'dp', axis=1, tiled=True)  31.4 us
    all_gather x1, blocking collectives, on_device(): lax.all_gather(w_value, 'dp', axis=1, tiled=True)  31.3 us
    all_gather x1, blocking collectives, on_device(): lax.all_gather(w_out, 'dp', axis=2, tiled=True)  27 us
  transfers between devices with their start and end apart: 6, of which 5 were waited for; matrix products, arithmetic and copies ran while one was open for 7% of the time, Pallas kernels for 0%

profile of v1, /device:TPU:0, one launch (start us, length us, event | category | flops | bytes accessed | tf_op | source)
XLA Modules:
  0.0 435.6 jit_solution(13901535496220445724)
XLA Ops:
  6.5 0.9 convert_element_type.339
  7.5 1.0 convert_reduce_fusion
  8.5 0.2 fusion.33
  8.7 0.8 fusion.212
  9.5 33.3 %all_gather.44 = bf16[2,1024,128]{2,1,0:T(8,128)(2,1)S(1)} all-gather(bf16[2,128,128]{2,1,0:T(8,128)(2,1)} %param.21), channel_id=1, replica_groups=mesh['dp'=8,'mp'=4] {'dp'}, dimensions={1}, use_global_device_ids=true | all-gather | bytes 589824 | tf_op jit(solution)/shard_map/all_gather | solution.py:52
  42.7 0.7 convert_element_type.341
  43.5 5.3 %fusion.3 = f32[2,8,256]{2,1,0:T(8,128)S(1)} fusion(bf16[2,8,256,1024]{3,2,1,0:T(8,128)(2,1)} %param.13, f32[8,1024]{1,0:T(8,128)S(1)} %convert_element_type.341), kind=kLoop, calls=%fused_computation.7 | loop fusion | flops 12578816 | bytes 8437760 | tf_op jit(solution)/shard_map/reduce_sum | solution.py:11
  48.7 0.5 copy-done
  49.2 3.2 multiply_reduce_fusion
  52.6 0.2 convolution_convert_fusion.10
  52.9 5.8 %multiply_convert_fusion = (bf16[2,8,256,1024]{3,2,1,0:T(8,128)(2,1)}, bf16[2,8,256,1024]{3,2,1,0:T(8,128)(2,1)S(1)}) fusion(bf16[2,8,256,1024]{3,2,1,0:T(8,128)(2,1)S(1)} %copy-done, f32[1024]{0:T(1024)S(1)} %bitcast.133, f32[2,8,256]{2,1,0:T(8,128)S(1)} %add_rsqrt_fusion, f32[2,8,256]{2,1,0:T(8,128)S(1)} %broadcast_multiply_fusion, ...), kind=kLoop, calls=%fused_computation.2 | loop fusion | flops 33554432 | bytes 25239552 | tf_op jit(solution)/shard_map/convert_element_type | solution.py:77
  58.6 3.5 convolution_convert_fusion.2
  62.1 31.3 %all_gather.42 = bf16[2,1024,128]{2,1,0:T(8,128)(2,1)S(1)} all-gather(bf16[2,128,128]{2,1,0:T(8,128)(2,1)S(1)} %copy-done.13), channel_id=1, replica_groups=mesh['dp'=8,'mp'=4] {'dp'}, dimensions={1}, use_global_device_ids=true | all-gather | bytes 589824 | tf_op jit(solution)/shard_map/all_gather | solution.py:53
  93.4 0.2 convolution_convert_fusion.11
  93.6 0.6 copy-done.4
  94.2 2.4 convolution_convert_fusion.3
  96.7 0.7 copy.29
  97.5 31.4 %all_gather.43 = bf16[2,1024,128]{2,1,0:T(8,128)(2,1)S(1)} all-gather(bf16[2,128,128]{2,1,0:T(8,128)(2,1)S(1)} %copy-done.14), channel_id=1, replica_groups=mesh['dp'=8,'mp'=4] {'dp'}, dimensions={1}, use_global_device_ids=true | all-gather | bytes 589824 | tf_op jit(solution)/shard_map/all_gather | solution.py:51
  128.9 0.2 fusion.17
  129.1 0.6 copy-done.11
  129.8 3.9 reshape.1028
  133.7 3.6 copy.28
  137.3 0.7 copy.26
  138.1 0.8 reshape.1027
  138.9 3.5 copy.25
  142.4 3.0 fusion.214
  145.4 2.2 fusion.15
  147.8 27.0 %all_gather.45 = bf16[2,128,1024]{2,1,0:T(8,128)(2,1)S(1)} all-gather(bf16[2,128,128]{2,1,0:T(8,128)(2,1)S(1)} %copy-done.15), channel_id=1, replica_groups=mesh['dp'=8,'mp'=4] {'dp'}, dimensions={2}, use_global_device_ids=true | all-gather | bytes 589824 | tf_op jit(solution)/shard_map/all_gather | solution.py:57
  174.9 0.8 copy-done.6
  175.7 0.9 convolution_convert_fusion.5
  176.7 0.7 all-gather.11.cloned.1.call-update
  177.5 0.7 all-gather.13.cloned.1.call-update
  178.2 14.9 %all-gather.15.cloned.1.call-done = bf16[512,1024]{1,0:T(8,128)(2,1)} async-done(((bf16[128,1024]{1,0:T(8,128)(2,1)}), bf16[512,1024]{1,0:T(8,128)(2,1)}) %all-gather.15.cloned.1.call-update) | async-done | bytes 1048592 | tf_op jit(solution)/shard_map/all_gather | solution.py:67
  193.2 1.4 reduce_sum.187
  194.7 0.2 multiply_reduce_fusion.4
  195.3 72.9 %all-gather.11.cloned.1.call-done = bf16[2,1024,1024]{2,1,0:T(8,128)(2,1)} async-done(((bf16[2,128,1024]{2,1,0:T(8,128)(2,1)}), bf16[2,1024,1024]{2,1,0:T(8,128)(2,1)}) %all-gather.11.cloned.1.call-update) | async-done | bytes 4194320 | tf_op jit(solution)/shard_map/all_gather | solution.py:54
  268.1 75.3 %all-gather.13.cloned.1.call-done = bf16[2,1024,1024]{2,1,0:T(8,128)(2,1)} async-done(((bf16[2,1024,128]{2,1,0:T(8,128)(2,1)}), bf16[2,1024,1024]{2,1,0:T(8,128)(2,1)}) %all-gather.13.cloned.1.call-update) | async-done | bytes 4194320 | tf_op jit(solution)/shard_map/all_gather | solution.py:58
  343.4 4.8 %fusion.13 = bf16[128,1024]{1,0:T(8,128)(2,1)} fusion(bf16[2,1024,1024]{2,1,0:T(8,128)(2,1)} %all-gather.13.cloned.1.call-done, bf16[128,1024]{1,0:T(8,128)(2,1)S(1)} %bitcast.127, bf16[2,1024,1024]{2,1,0:T(8,128)(2,1)} %all-gather.11.cloned.1.call-done), kind=kOutput, calls=%fused_computation.27 | convolution fusion | flops 545521664 | bytes 4718592 | tf_op jit(solution)/shard_map/dot_general | solution.py:17
  348.3 0.3 all-gather.19.cloned.1.call-start
  348.5 6.7 %convolution_convert_fusion = bf16[4096,128]{1,0:T(8,128)(2,1)} fusion(bf16[4096,1024]{1,0:T(8,128)(2,1)} %bitcast.110, bf16[2,1024,128]{2,1,0:T(8,128)(2,1)S(1)} %copy-done.2), kind=kOutput, calls=%fused_computation.9 | convolution fusion | flops 1074266112 | bytes 9699328 | tf_op jit(solution)/shard_map/dot_general | solution.py:17
  355.3 3.9 reshape.1030
  359.2 3.6 copy.36
  362.7 6.7 %convolution_convert_fusion.1 = bf16[4096,128]{1,0:T(8,128)(2,1)} fusion(bf16[4096,1024]{1,0:T(8,128)(2,1)} %bitcast.111, bf16[2,1024,128]{2,1,0:T(8,128)(2,1)} %copy-done.4), kind=kOutput, calls=%fused_computation.10 | convolution fusion | flops 1074266112 | bytes 9699328 | tf_op jit(solution)/shard_map/dot_general | solution.py:17
  369.4 3.9 reshape.1029
  373.3 3.5 copy.33
  376.8 1.5 reduce_sum.190
  378.5 0.2 multiply_reduce_fusion.3
  379.1 0.2 convolution_convert_fusion.8
  379.4 0.2 fusion.18
  379.6 0.2 convolution_convert_fusion.9
  380.3 3.2 fusion.219
  383.6 2.2 fusion.16
  386.0 0.9 convolution_convert_fusion.4
  387.0 0.3 all-gather.21.cloned.1.call-start
  387.3 14.8 %all-gather.19.cloned.1.call-done = bf16[512,1024]{1,0:T(8,128)(2,1)} async-done(((bf16[128,1024]{1,0:T(8,128)(2,1)}), bf16[512,1024]{1,0:T(8,128)(2,1)}) %all-gather.19.cloned.1.call-update) | async-done | bytes 1048592 | tf_op jit(solution)/shard_map/all_gather | solution.py:67
  402.1 1.4 reduce_sum.194
  403.5 0.2 fusion.210
  403.8 0.2 multiply_reduce_fusion.2
  404.1 0.2 multiply_convert_fusion.3
  404.3 4.8 %fusion.14 = bf16[128,1024]{1,0:T(8,128)(2,1)} fusion(bf16[2,1024,1024]{2,1,0:T(8,128)(2,1)} %all-gather.13.cloned.1.call-done, bf16[128,1024]{1,0:T(8,128)(2,1)S(1)} %bitcast.128, bf16[2,1024,1024]{2,1,0:T(8,128)(2,1)} %all-gather.11.cloned.1.call-done), kind=kOutput, calls=%fused_computation.28 | convolution fusion | flops 545521664 | bytes 4718592 | tf_op jit(solution)/shard_map/dot_general | solution.py:17
  409.1 16.8 %all-gather.21.cloned.1.call-done = bf16[512,1024]{1,0:T(8,128)(2,1)} async-done(((bf16[128,1024]{1,0:T(8,128)(2,1)}), bf16[512,1024]{1,0:T(8,128)(2,1)}) %all-gather.21.cloned.1.call-update) | async-done | bytes 1048592 | tf_op jit(solution)/shard_map/all_gather | solution.py:67
  425.9 1.4 reduce_sum.197
  427.5 0.2 multiply_reduce_fusion.1
  427.9 0.9 multiply_convert_fusion.2
  (85 shorter events, 3.1 us)
Async XLA Ops:
  6.5 186.6 %all-gather.15.cloned.1.call-start = ((), (), s32[]{:S(2)}) async-start(), calls=%async_computation.2 | async-start | bytes 1310720 | tf_op jit(solution)/shard_map/all_gather | solution.py:67
  42.7 15.9 %copy-start.1 = (bf16[2,1024,128]{2,1,0:T(8,128)(2,1)}, bf16[2,1024,128]{2,1,0:T(8,128)(2,1)S(1)}, u32[]{:S(2)}) copy-start(bf16[2,1024,128]{2,1,0:T(8,128)(2,1)S(1)} %all_gather.44) | copy-start | bytes 1572868
  43.5 5.8 %copy-start = (bf16[2,8,256,1024]{3,2,1,0:T(8,128)(2,1)S(1)}, bf16[2,8,256,1024]{3,2,1,0:T(8,128)(2,1)}, u32[]{:S(2)}) copy-start(bf16[2,8,256,1024]{3,2,1,0:T(8,128)(2,1)} %param.13) | copy-start | bytes 25165828
  49.2 3.2 copy-start.17
  58.6 3.5 copy-start.13
  93.4 0.8 copy-start.4
  94.2 3.2 copy-start.14
  128.9 0.8 copy-start.11
  138.9 3.5 copy-start.9
  142.4 3.0 copy-start.10
  142.4 3.0 copy-start.16
  145.4 2.4 copy-start.15
  147.6 30.6 %copy-start.18 = (f32[2,1024]{1,0:T(2,128)S(1)}, f32[2,1024]{1,0:T(2,128)}, u32[]{:S(2)}) copy-start(f32[2,1024]{1,0:T(2,128)} %param.18) | copy-start | bytes 24580
  174.9 0.8 copy-start.6
  176.7 91.5 %all-gather.11.cloned.1.call-start = ((), (), s32[]{:S(2)}) async-start(), calls=%async_computation | async-start | bytes 4718592 | tf_op jit(solution)/shard_map/all_gather | solution.py:54
  177.4 166.0 %all-gather.13.cloned.1.call-start = ((), (), s32[]{:S(2)}) async-start(), calls=%async_computation.1 | async-start | bytes 4718592 | tf_op jit(solution)/shard_map/all_gather | solution.py:58
  178.1 198.7 %all-gather.17.cloned.1.call-start = ((), (), s32[]{:S(2)}) async-start(), calls=%async_computation.3 | async-start | bytes 1310720 | tf_op jit(solution)/shard_map/all_gather | solution.py:67
  343.4 5.1 %copy-start.2 = (bf16[2,1024,128]{2,1,0:T(8,128)(2,1)S(1)}, bf16[2,1024,128]{2,1,0:T(8,128)(2,1)}, u32[]{:S(2)}) copy-start(bf16[2,1024,128]{2,1,0:T(8,128)(2,1)} %copy-done.1) | copy-start | bytes 1572868
  348.3 53.8 %all-gather.19.cloned.1.call-start = ((), (), s32[]{:S(2)}) async-start(), calls=%async_computation.4 | async-start | bytes 1310720 | tf_op jit(solution)/shard_map/all_gather | solution.py:67
  376.8 2.2 copy-start.3
  378.3 1.0 copy-start.12
  378.3 1.3 copy-start.5
  379.8 3.8 copy-start.8
  383.6 2.4 copy-start.7
  387.0 39.0 %all-gather.21.cloned.1.call-start = ((), (), s32[]{:S(2)}) async-start(), calls=%async_computation.5 | async-start | bytes 1310720 | tf_op jit(solution)/shard_map/all_gather | solution.py:67
  409.1 18.8 %copy-start.19 = (f32[1024]{0:T(1024)S(1)}, f32[1024]{0:T(1024)}, u32[]{:S(2)}) copy-start(f32[1024]{0:T(1024)} %param.19) | copy-start | bytes 12292
Sparse Core Ops, SparseCore 0:
  176.8 16.3 all-gather.14
  195.3 72.7 all-gather.10
  270.2 73.1 all-gather.12
  348.4 14.8 all-gather.16
  387.1 14.9 all-gather.18
  409.2 16.6 all-gather.20
